TPU v7x, 128 devices: a whole 4x4x4 slice. The times are simulated.
128 devices in a mesh: tok: 16 (over z, y_lo, core), feat: 8 (over y_hi, x).
Axes of the slice: x: 4, y: 4 (y_hi: 2, y_lo: 2; y = y_hi * 2 + y_lo), z: 4, core: 2. Of those that a mesh axis runs over, the one named last changes fastest.
Arguments:
- teacher: float32 [8192, 16384], P('tok', 'feat'), may hold values from -720 to 720, as said below
- student: float32 [8192, 2048], P('tok', 'feat'), may hold values from -6 to 6
- gain: float32 [16384], P('feat'), may hold values from 0.1 to 1.9
- projector: float32 [2048, 16384], P(None, 'feat'), may hold values from -0.1875 to 0.1875
- momentum: float32 [2048, 16384], P('tok', 'feat'), may hold values from -0.12 to 0.12
Outputs:
- new_projector: float32 [2048, 16384], P('tok', 'feat')
- new_momentum: float32 [2048, 16384], P('tok', 'feat')
- student_grad: float32 [8192, 2048], P('tok', 'feat')
- loss_value: float32 [], replicated
Inputs may be any that keep to these rules, and one draw needn't show every extreme that they name: `teacher`: finite real values.
All inputs are finite; a program needn't handle non-finite values.
Results may differ from a plain program's by a relative error of at most 0.00011.
Values sent between devices are 32-bit elements; how exact they have to be, the bound alone decides.
No kernel may reach another device: no remote copies, remote signals or barrier semaphores. Data moves between devices by JAX's collectives and lax.ppermute only.
A program may use at most 128 MiB of HBM per device.

v0:
```python
import jax
import jax.numpy as jnp
from jax import lax
from jax.sharding import Mesh
from jax.sharding import PartitionSpec as P

DT = 16384
TOK = ("tok_0", "tok_1", "tok_2")
FEAT = ("feat_0", "feat_1")
TOK_FEAT = ("tok_0", "tok_1", "tok_2", "feat_0", "feat_1")
norm_eps = 1e-05
momentum_rate = 0.9
step_rate = 0.5


def over_axes(value, axes):
    for axis in axes:
        value = lax.psum(value, axis)
    return value


def split_up(value, dim, devices):
    before, after = (value.shape[:dim], value.shape[dim + 1 :])
    return jnp.moveaxis(value.reshape(*before, devices, -1, *after), dim, 0)


def summed_on_arrival(value, axis, dim):
    blocks = split_up(value, dim, lax.axis_size(axis))
    arrived = lax.all_to_all(blocks, axis, split_axis=0, concat_axis=0, tiled=True)
    return arrived.sum(axis=0)


def on_device(teacher, student, gain, projector, momentum):
    highest = lax.Precision.HIGHEST
    local_rows = teacher.shape[0]
    token_count = local_rows * lax.axis_size(TOK)
    full_student = lax.all_gather(student, FEAT, axis=1, tiled=True)
    predicted = jnp.dot(
        full_student, projector, precision=highest, preferred_element_type=jnp.float32
    )
    weighted = teacher * gain[None, :]
    squares_part = jnp.sum(teacher * teacher, axis=1)
    row_total = lax.psum(squares_part, FEAT)
    row_scale = lax.rsqrt(row_total / DT + norm_eps)
    residual = predicted - weighted * row_scale[:, None]
    error_sum = over_axes(jnp.sum(residual * residual), TOK_FEAT)
    loss_value = error_sum / (token_count * DT)
    own_count = projector.shape[0] // lax.axis_size(TOK)
    proj_grad = lax.psum_scatter(
        lax.dot_general(
            full_student,
            residual,
            (((0,), (0,)), ((), ())),
            precision=highest,
            preferred_element_type=jnp.float32,
        )
        / token_count,
        TOK,
        scatter_dimension=0,
        tiled=True,
    )
    student_terms = lax.dot_general(
        residual,
        projector,
        (((1,), (1,)), ((), ())),
        precision=highest,
        preferred_element_type=jnp.float32,
    )
    student_grad = summed_on_arrival(student_terms, FEAT, 1)
    new_momentum = momentum_rate * momentum + proj_grad
    first_own = lax.axis_index(TOK) * own_count
    own_rows = lax.dynamic_slice_in_dim(projector, first_own, own_count, 0)
    new_projector = own_rows - step_rate * new_momentum
    return (new_projector, new_momentum, student_grad, loss_value)


def solution(mesh):
    split = Mesh(
        mesh.devices.reshape(4, 2, 2, 2, 4), ("tok_0", "tok_1", "tok_2", "feat_0", "feat_1")
    )
    in_specs = (P(TOK, FEAT), P(TOK, FEAT), P(FEAT), P(None, FEAT), P(TOK, FEAT))
    out_specs = (P(TOK, FEAT), P(TOK, FEAT), P(TOK, FEAT), P())
    return jax.shard_map(
        on_device, mesh=split, in_specs=in_specs, out_specs=out_specs, check_vma=False
    )
```

profile of v0, /device:TPU:0, one launch (start us, length us, event | category | flops | bytes accessed | tf_op | source)
XLA Modules:
  0.0 395.2 jit_solution(3353362954193325163)
XLA Ops:
  7.2 0.0 copy-start.4
  7.2 0.0 all-gather.2.cloned.1.call-start
  7.2 0.7 all-gather.2.cloned.1.call-update
  7.9 0.0 reduce-scatter.2.cloned.1.call-start
  8.0 2.5 multiply_reduce_fusion
  10.5 24.6 %psum.42 = f32[512]{0:T(512)S(1)} all-reduce(f32[512]{0:T(512)S(1)} %multiply_reduce_fusion), channel_id=1, replica_groups=mesh['tok_0'=4,'tok_1'=2,'tok_2'=2,'feat_0'=2,'feat_1'=4] {'feat_0','fea..., use_global_device_ids=true, to_apply=%region_1.0 | all-reduce | flops 512 | bytes 4096 | tf_op jit(solution)/shard_map/psum | solution.py:43
  35.1 54.8 %all-gather.2.cloned.1.call-done = f32[512,2048]{1,0:T(8,128)} async-done(((f32[512,256]{1,0:T(8,128)}), f32[512,2048]{1,0:T(8,128)}) %all-gather.2.cloned.1.call-update) | async-done | bytes 4194320 | tf_op jit(solution)/shard_map/all_gather | solution.py:37
  89.9 0.0 copy-done.4
  89.9 32.5 %fusion.6 = (f32[]{:T(128)}, f32[512,2048]{1,0:T(8,128)S(1)}) fusion(f32[512,2048]{1,0:T(8,128)} %param.5, f32[512]{0:T(512)S(1)} %add_rsqrt_fusion, f32[2048]{0:T(1024)S(1)} %copy-done.4, f32[512,2048]{1,0:T(8,128)} %all-gather.2.cloned.1.call-done, f32[2048,2048]{1,0:T(8,128)} %param.8), kind=kOutput, calls=%fused_computation.6 | convolution fusion | flops 25775046656 | bytes 29370372 | tf_op jit(solution)/shard_map/dot_general | solution.py:38
  122.4 1.9 copy-done.1
  124.3 0.0 copy-done
  124.3 0.0 copy-done.2
  124.3 30.1 %multiply_bitcast_fusion = f32[2048,2048]{0,1:T(8,128)} fusion(f32[512,2048]{1,0:T(8,128)S(1)} %copy-done.2, f32[512,2048]{1,0:T(8,128)S(1)} %get-tuple-element.15, f32[512,2048]{1,0:T(8,128)S(1)} %copy-done, f32[512]{0:T(512)S(1)} %add_rsqrt_fusion, f32[2048]{0:T(1024)S(1)} %copy-done.4), kind=kOutput, calls=%fused_computation | convolution fusion | flops 25777143808 | bytes 29370368 | tf_op jit(solution)/shard_map/dot_general | solution.py:50
  154.4 0.0 reduce-scatter.2.cloned.1.call-update
  154.5 32.0 %fusion = f32[512,2048]{1,0:T(8,128)S(1)} fusion(f32[2048,2048]{1,0:T(8,128)} %param.8, f32[512,2048]{1,0:T(8,128)} %copy-done.1, f32[512,2048]{1,0:T(8,128)} %param.5, f32[512]{0:T(512)S(1)} %add_rsqrt_fusion, f32[2048]{0:T(1024)S(1)} %copy-done.4), kind=kOutput, calls=%fused_computation.2 | convolution fusion | flops 25772949504 | bytes 29370368 | tf_op jit(solution)/shard_map/dot_general | solution.py:62
  186.5 2.4 copy.21
  188.8 4.5 %all-to-all-start = ((f32[8,512,256]{2,1,0:T(8,128)}), f32[8,512,256]{2,1,0:T(8,128)}, u32[]{:S(2)}, u32[]{:S(2)}) async-start(f32[8,512,256]{2,1,0:T(8,128)} %bitcast.13), calls=%async_computation.1 | async-start | bytes 8388608 | tf_op jit(solution)/shard_map/all_to_all | solution.py:29
  193.4 0.0 copy-start.3
  193.4 11.3 %psum.43 = f32[]{:T(128)} all-reduce(f32[]{:T(128)} %get-tuple-element.14), channel_id=1, replica_groups=mesh['tok_0'=4,'tok_1'=2,'tok_2'=2,'feat_0'=2,'feat_1'=4] {'tok_0'}, use_global_device_ids=true, to_apply=%region_5.0 | all-reduce | flops 1 | bytes 8 | tf_op jit(solution)/shard_map/psum | solution.py:18
  204.8 47.1 %psum.44 = f32[]{:T(128)} all-reduce(f32[]{:T(128)} %psum.43), channel_id=1, replica_groups=mesh['tok_0'=4,'tok_1'=2,'tok_2'=2,'feat_0'=2,'feat_1'=4] {'tok_1'}, use_global_device_ids=true, to_apply=%region_6.0 | all-reduce | flops 1 | bytes 8 | tf_op jit(solution)/shard_map/psum | solution.py:18
  251.9 1.3 constant_dynamic-slice_fusion
  253.2 3.1 psum.45
  256.3 0.3 copy.18
  256.6 7.8 %psum.46 = f32[]{:T(128)} all-reduce(f32[]{:T(128)} %psum.45), channel_id=1, replica_groups=mesh['tok_0'=4,'tok_1'=2,'tok_2'=2,'feat_0'=2,'feat_1'=4] {'feat_0'}, use_global_device_ids=true, to_apply=%region_8.0 | all-reduce | flops 1 | bytes 8 | tf_op jit(solution)/shard_map/psum | solution.py:18
  264.4 0.3 copy.14
  264.7 9.8 %psum.47 = f32[]{:T(128)} all-reduce(f32[]{:T(128)} %psum.46), channel_id=1, replica_groups=mesh['tok_0'=4,'tok_1'=2,'tok_2'=2,'feat_0'=2,'feat_1'=4] {'feat_1'}, use_global_device_ids=true, to_apply=%region_9.0 | all-reduce | flops 1 | bytes 8 | tf_op jit(solution)/shard_map/psum | solution.py:18
  275.2 0.0 all-to-all-done
  275.2 3.3 reduce_sum.28
  278.6 102.5 %reduce-scatter.2.cloned.1.call-done = f32[128,2048]{0,1:T(8,128)} async-done(((f32[2048,2048]{0,1:T(8,128)}), f32[128,2048]{0,1:T(8,128)}) %reduce-scatter.2.cloned.1.call-update) | async-done | bytes 1048592 | tf_op jit(solution)/shard_map/reduce_scatter | solution.py:49
  381.0 2.4 multiply_subtract_fusion
  383.4 2.5 copy.16
  385.9 1.3 copy.17
  (5 shorter events, 0.0 us)
Async XLA Ops:
  7.2 82.7 %copy-start.4 = (f32[2048]{0:T(1024)S(1)}, f32[2048]{0:T(1024)}, u32[]{:S(2)}) copy-start(f32[2048]{0:T(1024)} %param.7) | copy-start | bytes 24580
  7.2 82.7 %all-gather.2.cloned.1.call-start = ((), (), s32[]{:S(2)}) async-start(), calls=%async_computation.2 | async-start | bytes 4718592 | tf_op jit(solution)/shard_map/all_gather | solution.py:37
  7.9 373.1 %reduce-scatter.2.cloned.1.call-start = ((), (), s32[]{:S(2)}) async-start(), calls=%async_computation.3 | async-start | bytes 17825792 | tf_op jit(solution)/shard_map/reduce_scatter | solution.py:49
  89.9 34.5 %copy-start = (f32[512,2048]{1,0:T(8,128)S(1)}, f32[512,2048]{1,0:T(8,128)}, u32[]{:S(2)}) copy-start(f32[512,2048]{1,0:T(8,128)} %param.5) | copy-start | bytes 12582916
  89.9 34.5 %copy-start.2 = (f32[512,2048]{1,0:T(8,128)S(1)}, f32[512,2048]{1,0:T(8,128)}, u32[]{:S(2)}) copy-start(f32[512,2048]{1,0:T(8,128)} %all-gather.2.cloned.1.call-done) | copy-start | bytes 12582916
  122.4 1.9 copy-start.1
  188.8 86.4 %all-to-all-start = ((f32[8,512,256]{2,1,0:T(8,128)}), f32[8,512,256]{2,1,0:T(8,128)}, u32[]{:S(2)}, u32[]{:S(2)}) async-start(f32[8,512,256]{2,1,0:T(8,128)} %bitcast.13), calls=%async_computation.1 | async-start | bytes 8388608 | tf_op jit(solution)/shard_map/all_to_all | solution.py:29
  193.4 71.0 %copy-start.3 = (f32[128,2048]{1,0:T(8,128)S(1)}, f32[128,2048]{1,0:T(8,128)}, u32[]{:S(2)}) copy-start(f32[128,2048]{1,0:T(8,128)} %param.9) | copy-start | bytes 3145732
Sparse Core Ops, SparseCore 0:
  10.2 79.6 all-gather.1
  154.6 226.3 reduce-scatter.1
where the time goes:
time: 396 us; the launch traced here: 395 us
  waiting for transfers between devices  158 us (40%)
  blocking collectives  104 us (26%)
  matrix products  94.6 us (24%)
  between operations  15.9 us (4%)
  local copies, waits for them, and re-layouts  10.1 us (3%)
  other arithmetic  8.28 us (2%)
  starting transfers between devices  4.62 us (1%)
    reduce_scatter x1, waiting for transfers between devices, on_device(): lax.psum_scatter(lax.dot_general(full_student, residual, (((0,), (0,)), (...  102 us
    psum x5, blocking collectives, over_axes(): value = lax.psum(value, axis)  79.2 us
    all_gather x1, waiting for transfers between devices, on_device(): full_student = lax.all_gather(student, FEAT, axis=1, tiled=True)  54.8 us
    dot_general x1, matrix products, on_device(): jnp.dot(full_student, projector, precision=highest, preferred_element_typ...  32.5 us
    dot_general x1, matrix products, on_device(): lax.dot_general(residual, projector, (((1,), (1,)), ((), ())), precision=...  32 us
    dot_general x1, matrix products, on_device(): lax.dot_general(full_student, residual, (((0,), (0,)), ((), ())), precisi...  30.1 us
    psum x1, blocking collectives, on_device(): row_total = lax.psum(squares_part, FEAT)  24.6 us
  transfers between devices with their start and end apart: 3, of which 2 were waited for; matrix products, arithmetic and copies ran while one was open for 11% of the time, Pallas kernels for 0%

commit v1 on v0

--- a/solution.py
+++ b/solution.py
@@ -40,7 +40,7 @@
     )
     weighted = teacher * gain[None, :]
     squares_part = jnp.sum(teacher * teacher, axis=1)
-    row_total = lax.psum(squares_part, FEAT)
+    row_total = lax.psum(lax.psum(squares_part, "feat_1"), "feat_0")
     row_scale = lax.rsqrt(row_total / DT + norm_eps)
     residual = predicted - weighted * row_scale[:, None]
     error_sum = over_axes(jnp.sum(residual * residual), TOK_FEAT)

time: 396 us -> 396 us (level)
  blocking collectives: 104 us -> 96.2 us
  waiting for transfers between devices: 158 us -> 165 us
    psum x1 -> x2, blocking collectives: 24.6 us -> 17 us  [on_device(): row_total = lax.psum(lax.psum(squares_part, 'feat_1'), 'feat_0')]
    all_gather x1, waiting for transfers between devices: 54.8 us -> 62.3 us  [on_device(): full_student = lax.all_gather(student, FEAT, axis=1, tiled=True)]
where the time goes in v1:
time: 396 us; the launch traced here: 395 us
  waiting for transfers between devices  165 us (42%)
  blocking collectives  96.2 us (24%)
  matrix products  94.6 us (24%)
  between operations  15.9 us (4%)
  local copies, waits for them, and re-layouts  10.1 us (3%)
  other arithmetic  8.28 us (2%)
  starting transfers between devices  4.62 us (1%)
    reduce_scatter x1, waiting for transfers between devices, on_device(): lax.psum_scatter(lax.dot_general(full_student, residual, (((0,), (0,)), (...  102 us
    psum x5, blocking collectives, over_axes(): value = lax.psum(value, axis)  79.2 us
    all_gather x1, waiting for transfers between devices, on_device(): full_student = lax.all_gather(student, FEAT, axis=1, tiled=True)  62.3 us
    dot_general x1, matrix products, on_device(): jnp.dot(full_student, projector, precision=highest, preferred_element_typ...  32.5 us
    dot_general x1, matrix products, on_device(): lax.dot_general(residual, projector, (((1,), (1,)), ((), ())), precision=...  32 us
    dot_general x1, matrix products, on_device(): lax.dot_general(full_student, residual, (((0,), (0,)), ((), ())), precisi...  30.1 us
    psum x2, blocking collectives, on_device(): row_total = lax.psum(lax.psum(squares_part, 'feat_1'), 'feat_0')  17 us
  transfers between devices with their start and end apart: 3, of which 2 were waited for; matrix products, arithmetic and copies ran while one was open for 11% of the time, Pallas kernels for 0%

profile of v1, /device:TPU:0, one launch (start us, length us, event | category | flops | bytes accessed | tf_op | source)
XLA Modules:
  0.0 395.1 jit_solution(377545476042672960)
XLA Ops:
  7.2 0.0 copy-start.4
  7.2 0.0 all-gather.2.cloned.1.call-start
  7.2 0.7 all-gather.2.cloned.1.call-update
  7.9 0.0 reduce-scatter.2.cloned.1.call-start
  8.0 2.5 multiply_reduce_fusion
  10.5 10.6 %psum.49 = f32[512]{0:T(512)S(1)} all-reduce(f32[512]{0:T(512)S(1)} %multiply_reduce_fusion), channel_id=1, replica_groups=mesh['tok_0'=4,'tok_1'=2,'tok_2'=2,'feat_0'=2,'feat_1'=4] {'feat_1'}, use_global_device_ids=true, to_apply=%region_1.0 | all-reduce | flops 512 | bytes 4096 | tf_op jit(solution)/shard_map/psum | solution.py:43
  21.1 6.4 %psum.50 = f32[512]{0:T(512)S(1)} all-reduce(f32[512]{0:T(512)S(1)} %psum.49), channel_id=1, replica_groups=mesh['tok_0'=4,'tok_1'=2,'tok_2'=2,'feat_0'=2,'feat_1'=4] {'feat_0'}, use_global_device_ids=true, to_apply=%region_2.0 | all-reduce | flops 512 | bytes 4096 | tf_op jit(solution)/shard_map/psum | solution.py:43
  27.5 62.3 %all-gather.2.cloned.1.call-done = f32[512,2048]{1,0:T(8,128)} async-done(((f32[512,256]{1,0:T(8,128)}), f32[512,2048]{1,0:T(8,128)}) %all-gather.2.cloned.1.call-update) | async-done | bytes 4194320 | tf_op jit(solution)/shard_map/all_gather | solution.py:37
  89.8 0.0 copy-done.4
  89.8 32.5 %fusion.6 = (f32[]{:T(128)}, f32[512,2048]{1,0:T(8,128)S(1)}) fusion(f32[512,2048]{1,0:T(8,128)} %param.5, f32[512]{0:T(512)S(1)} %add_rsqrt_fusion, f32[2048]{0:T(1024)S(1)} %copy-done.4, f32[512,2048]{1,0:T(8,128)} %all-gather.2.cloned.1.call-done, f32[2048,2048]{1,0:T(8,128)} %param.8), kind=kOutput, calls=%fused_computation.6 | convolution fusion | flops 25775046656 | bytes 29370372 | tf_op jit(solution)/shard_map/dot_general | solution.py:38
  122.3 1.9 copy-done.1
  124.2 0.0 copy-done.2
  124.3 30.1 %multiply_bitcast_fusion = f32[2048,2048]{0,1:T(8,128)} fusion(f32[512,2048]{1,0:T(8,128)S(1)} %copy-done.2, f32[512,2048]{1,0:T(8,128)S(1)} %get-tuple-element.15, f32[512,2048]{1,0:T(8,128)S(1)} %copy-done, f32[512]{0:T(512)S(1)} %add_rsqrt_fusion, f32[2048]{0:T(1024)S(1)} %copy-done.4), kind=kOutput, calls=%fused_computation | convolution fusion | flops 25777143808 | bytes 29370368 | tf_op jit(solution)/shard_map/dot_general | solution.py:50
  154.4 0.0 reduce-scatter.2.cloned.1.call-update
  154.4 32.0 %fusion = f32[512,2048]{1,0:T(8,128)S(1)} fusion(f32[2048,2048]{1,0:T(8,128)} %param.8, f32[512,2048]{1,0:T(8,128)} %copy-done.1, f32[512,2048]{1,0:T(8,128)} %param.5, f32[512]{0:T(512)S(1)} %add_rsqrt_fusion, f32[2048]{0:T(1024)S(1)} %copy-done.4), kind=kOutput, calls=%fused_computation.2 | convolution fusion | flops 25772949504 | bytes 29370368 | tf_op jit(solution)/shard_map/dot_general | solution.py:62
  186.4 2.4 copy.21
  188.7 4.5 %all-to-all-start = ((f32[8,512,256]{2,1,0:T(8,128)}), f32[8,512,256]{2,1,0:T(8,128)}, u32[]{:S(2)}, u32[]{:S(2)}) async-start(f32[8,512,256]{2,1,0:T(8,128)} %bitcast.13), calls=%async_computation.1 | async-start | bytes 8388608 | tf_op jit(solution)/shard_map/all_to_all | solution.py:29
  193.3 0.0 copy-start.3
  193.3 11.4 %psum.51 = f32[]{:T(128)} all-reduce(f32[]{:T(128)} %get-tuple-element.14), channel_id=1, replica_groups=mesh['tok_0'=4,'tok_1'=2,'tok_2'=2,'feat_0'=2,'feat_1'=4] {'tok_0'}, use_global_device_ids=true, to_apply=%region_6.0 | all-reduce | flops 1 | bytes 8 | tf_op jit(solution)/shard_map/psum | solution.py:18
  204.7 47.1 %psum.52 = f32[]{:T(128)} all-reduce(f32[]{:T(128)} %psum.51), channel_id=1, replica_groups=mesh['tok_0'=4,'tok_1'=2,'tok_2'=2,'feat_0'=2,'feat_1'=4] {'tok_1'}, use_global_device_ids=true, to_apply=%region_7.0 | all-reduce | flops 1 | bytes 8 | tf_op jit(solution)/shard_map/psum | solution.py:18
  251.8 1.3 constant_dynamic-slice_fusion
  253.1 3.1 psum.53
  256.2 0.3 copy.18
  256.5 7.8 %psum.54 = f32[]{:T(128)} all-reduce(f32[]{:T(128)} %psum.53), channel_id=1, replica_groups=mesh['tok_0'=4,'tok_1'=2,'tok_2'=2,'feat_0'=2,'feat_1'=4] {'feat_0'}, use_global_device_ids=true, to_apply=%region_9.0 | all-reduce | flops 1 | bytes 8 | tf_op jit(solution)/shard_map/psum | solution.py:18
  264.3 0.3 copy.14
  264.6 9.8 %psum.55 = f32[]{:T(128)} all-reduce(f32[]{:T(128)} %psum.54), channel_id=1, replica_groups=mesh['tok_0'=4,'tok_1'=2,'tok_2'=2,'feat_0'=2,'feat_1'=4] {'feat_1'}, use_global_device_ids=true, to_apply=%region_10.0 | all-reduce | flops 1 | bytes 8 | tf_op jit(solution)/shard_map/psum | solution.py:18
  275.1 0.0 all-to-all-done
  275.1 3.3 reduce_sum.28
  278.5 102.5 %reduce-scatter.2.cloned.1.call-done = f32[128,2048]{0,1:T(8,128)} async-done(((f32[2048,2048]{0,1:T(8,128)}), f32[128,2048]{0,1:T(8,128)}) %reduce-scatter.2.cloned.1.call-update) | async-done | bytes 1048592 | tf_op jit(solution)/shard_map/reduce_scatter | solution.py:49
  380.9 2.4 multiply_subtract_fusion
  383.3 2.5 copy.16
  385.8 1.3 copy.17
  (6 shorter events, 0.0 us)
Async XLA Ops:
  7.2 82.6 %copy-start.4 = (f32[2048]{0:T(1024)S(1)}, f32[2048]{0:T(1024)}, u32[]{:S(2)}) copy-start(f32[2048]{0:T(1024)} %param.7) | copy-start | bytes 24580
  7.2 82.6 %all-gather.2.cloned.1.call-start = ((), (), s32[]{:S(2)}) async-start(), calls=%async_computation.2 | async-start | bytes 4718592 | tf_op jit(solution)/shard_map/all_gather | solution.py:37
  7.9 373.0 %reduce-scatter.2.cloned.1.call-start = ((), (), s32[]{:S(2)}) async-start(), calls=%async_computation.3 | async-start | bytes 17825792 | tf_op jit(solution)/shard_map/reduce_scatter | solution.py:49
  89.8 34.5 %copy-start = (f32[512,2048]{1,0:T(8,128)S(1)}, f32[512,2048]{1,0:T(8,128)}, u32[]{:S(2)}) copy-start(f32[512,2048]{1,0:T(8,128)} %param.5) | copy-start | bytes 12582916
  89.8 34.5 %copy-start.2 = (f32[512,2048]{1,0:T(8,128)S(1)}, f32[512,2048]{1,0:T(8,128)}, u32[]{:S(2)}) copy-start(f32[512,2048]{1,0:T(8,128)} %all-gather.2.cloned.1.call-done) | copy-start | bytes 12582916
  122.3 1.9 copy-start.1
  188.7 86.4 %all-to-all-start = ((f32[8,512,256]{2,1,0:T(8,128)}), f32[8,512,256]{2,1,0:T(8,128)}, u32[]{:S(2)}, u32[]{:S(2)}) async-start(f32[8,512,256]{2,1,0:T(8,128)} %bitcast.13), calls=%async_computation.1 | async-start | bytes 8388608 | tf_op jit(solution)/shard_map/all_to_all | solution.py:29
  193.3 71.0 %copy-start.3 = (f32[128,2048]{1,0:T(8,128)S(1)}, f32[128,2048]{1,0:T(8,128)}, u32[]{:S(2)}) copy-start(f32[128,2048]{1,0:T(8,128)} %param.9) | copy-start | bytes 3145732
Sparse Core Ops, SparseCore 0:
  10.2 79.5 all-gather.1
  154.5 226.3 reduce-scatter.1
